TPU v7x, 256 devices: a whole 4x4x8 slice. The times are simulated.
256 devices in a mesh: expert: 8 (over x, core), context: 32 (over y, z).
Axes of the slice: x: 4, y: 4, z: 8, core: 2. Of those that a mesh axis runs over, the one named last changes fastest.
Arguments:
- hidden: bfloat16 [8, 4096, 2048], P('expert', 'context'), may hold values from -6 to 6
- query: bfloat16 [8, 4096, 2048], P('expert', 'context'), may hold values from -120 to 120
- keys: bfloat16 [8, 4096, 512], P('expert', 'context'), may hold values from -6 to 6
- values: bfloat16 [8, 4096, 512], P('expert', 'context'), may hold values from -6 to 6
- x_inner: bfloat16 [8, 4096, 4096], P('expert', 'context'), may hold values from -6 to 6
- z_gate: bfloat16 [8, 4096, 4096], P('expert', 'context'), may hold values from -6 to 6
- dt_raw: bfloat16 [8, 4096, 4096], P('expert', 'context'), may hold values from -5 to 5
- b_proj: float32 [8, 4096, 16], P('expert', 'context'), may hold values from -0.6 to 0.6
- c_proj: float32 [8, 4096, 16], P('expert', 'context'), may hold values from -0.6 to 0.6
- conv_weight: float32 [4, 4096], replicated, may hold values from -3 to 3
- conv_bias: float32 [4096], replicated, may hold values from -3 to 3
- dt_bias: float32 [4096], replicated, may hold values from -0.5 to 0.5
- a_rate: float32 [16, 4096], replicated, may hold values from 7.324219e-05 to 0.05
- skip_gain: float32 [4096], replicated, may hold values from 0.5 to 1.5
- mamba_vector: float32 [4096], replicated, may hold values from -0.09375 to 0.09375
- attn_vector: float32 [2048], replicated, may hold values from -0.125 to 0.125
- impact_vector: float32 [2048], replicated, may hold values from -0.125 to 0.125
- norm_gain: float32 [2048], replicated, may hold values from 0.5 to 1.5
- expert_gate: bfloat16 [16, 2048, 7168], P('expert', None, 'context'), may hold values from -0.125 to 0.125
- expert_up: bfloat16 [16, 2048, 7168], P('expert', None, 'context'), may hold values from -0.125 to 0.125
- expert_vector: float32 [16, 7168], P('expert', 'context'), may hold values from -0.0625 to 0.0625
- routes: int32 [8, 4096, 2], P('expert', 'context'), may hold values from 0 to 15, all different within a row
- route_gate: float32 [8, 4096, 2], P('expert', 'context'), may hold values from 0.1 to 0.9
- lengths: int32 [8], replicated, may hold values from 1 to 4096, 20480 in all
- term_ids: int32 [8, 4096], P('expert', 'context'), may hold values from 0 to 65535
Outputs:
- token_impacts: float32 [8, 4096], P('expert', 'context')
- term_impacts: float32 [8, 65536], P('expert', 'context')
All inputs are finite; a program needn't handle non-finite values.
Results may differ from a plain program's by a relative error of at most 0.009.
Values may be sent and summed in bfloat16 or wider, within the bound.
A program may use at most 192 MiB of HBM per device.

v0:
```python
import jax
import jax.numpy as jnp
from jax import lax
from jax.sharding import PartitionSpec as P

H = 16
HD = 128
KVH = 4
KCONV = 4
VOCAB = 65536
big_negative = -1e30
norm_eps = 1e-06


def passed_along(x, axis, by):
    devices = lax.axis_size(axis)
    pairs = [(i, i + by) for i in range(devices) if 0 <= i + by < devices]
    return lax.ppermute(x, axis, pairs)


def prefix(x, axis, join, neutral):
    place = lax.axis_index(axis)
    gathered = jax.tree.map(
        lambda a, kind: lax.all_gather(a.astype(kind), axis), x, (jnp.bfloat16, jnp.bfloat16)
    )
    state = jax.tree.map(lambda a, e: jnp.zeros_like(a) + jnp.asarray(e, a.dtype), x, neutral)

    def one(turn, state):
        return join(
            state,
            jax.tree.map(
                lambda a, own: lax.dynamic_index_in_dim(a, turn, 0, False).astype(own.dtype),
                gathered,
                x,
            ),
        )

    return lax.fori_loop(0, place, one, state)


def shards(
    hidden,
    query,
    keys,
    values,
    x_inner,
    z_gate,
    dt_raw,
    b_proj,
    c_proj,
    conv_weight,
    conv_bias,
    dt_bias,
    a_rate,
    skip_gain,
    mamba_vector,
    attn_vector,
    impact_vector,
    norm_gain,
    expert_gate,
    expert_up,
    expert_vector,
    routes,
    route_gate,
    lengths,
    term_ids,
):
    tokens_here = hidden.shape[1]
    doc_index = lax.axis_index("expert")
    shard_index = lax.axis_index("context")
    doc_length = lax.dynamic_index_in_dim(lengths, doc_index, 0, False)
    positions = shard_index * tokens_here + jnp.arange(tokens_here, dtype=jnp.int32)
    live_rows = positions < doc_length
    groups = H // KVH
    score_scale = HD ** (-0.5)
    queries = query[0].reshape(tokens_here, KVH, groups, HD)

    def key_block(carried, kv_block, first_key):
        running_max, running_sum, running_out = carried
        key_rows, value_rows = kv_block
        block_width = key_rows.shape[0]
        key_heads = key_rows.reshape(block_width, KVH, HD)
        value_heads = value_rows.reshape(block_width, KVH, HD)
        scores = (
            jnp.einsum("tgqd,rgd->gqtr", queries, key_heads, preferred_element_type=jnp.float32)
            * score_scale
        )
        key_positions = first_key + jnp.arange(block_width, dtype=jnp.int32)
        allowed = key_positions[None, :] <= positions[:, None]
        scores = jnp.where(allowed, scores, big_negative)
        new_max = jnp.maximum(running_max, jnp.max(scores, axis=-1))
        exp_scores = jnp.where(allowed, jnp.exp(scores - new_max[..., None]), 0.0)
        factor = jnp.exp(running_max - new_max)
        running_sum = running_sum * factor + jnp.sum(exp_scores, axis=-1)
        running_out = running_out * factor[..., None] + jnp.einsum(
            "gqtr,rgd->gqtd",
            exp_scores.astype(jnp.bfloat16),
            value_heads,
            preferred_element_type=jnp.float32,
        )
        return (new_max, running_sum, running_out)

    start_state = (
        jnp.full((KVH, groups, tokens_here), big_negative, jnp.float32),
        jnp.zeros((KVH, groups, tokens_here), jnp.float32),
        jnp.zeros((KVH, groups, tokens_here, HD), jnp.float32),
    )
    key_piece = lax.all_gather(keys[0], "context", axis=0, tiled=True)
    value_piece = lax.all_gather(values[0], "context", axis=0, tiled=True)
    piece_rows = key_piece.shape[0]
    block_rows = 512

    def one_block(inner_state, offset):
        kv_block = (
            lax.dynamic_slice_in_dim(key_piece, offset, block_rows, 0),
            lax.dynamic_slice_in_dim(value_piece, offset, block_rows, 0),
        )
        updated = key_block(inner_state, kv_block, offset)
        return (updated, None)

    offsets = jnp.arange(0, piece_rows, block_rows, dtype=jnp.int32)
    final_state = lax.scan(one_block, start_state, offsets)[0]
    running_sum = final_state[1]
    attended = final_state[2] / jnp.where(running_sum > 0.0, running_sum, 1.0)[..., None]
    attended = (
        jnp.transpose(attended, (2, 0, 1, 3)).reshape(tokens_here, H * HD).astype(jnp.bfloat16)
    )
    attn_score = jnp.sum(attended.astype(jnp.float32) * attn_vector[None, :], axis=-1)
    inner_rows = x_inner[0]
    conv_rim = passed_along(inner_rows[tokens_here - (KCONV - 1) :], "context", 1)
    extended = jnp.concatenate([conv_rim, inner_rows], axis=0).astype(jnp.float32)
    conv_sum = conv_bias[None, :]
    for tap_index in range(KCONV):
        conv_sum = (
            conv_sum
            + conv_weight[tap_index][None, :] * extended[tap_index : tap_index + tokens_here]
        )
    conved = jax.nn.silu(conv_sum)
    step_size = jax.nn.softplus(dt_raw[0].astype(jnp.float32) + dt_bias[None, :])
    neg_rate = -a_rate
    b_rows = b_proj[0]
    c_rows = c_proj[0]

    def emit_rows(carried, per_step):
        size_now, b_now, c_now, x_now = per_step
        carried = (
            jnp.exp(size_now[None, :] * neg_rate) * carried
            + (size_now * x_now)[None, :] * b_now[:, None]
        )
        return (carried, jnp.sum(c_now[:, None] * carried, axis=0))

    zero_state = jnp.zeros(a_rate.shape, jnp.float32)
    local_end, local_outputs = lax.scan(emit_rows, zero_state, (step_size, b_rows, c_rows, conved))
    cumulative = jnp.cumsum(step_size, axis=0)
    through = jnp.exp(neg_rate * cumulative[tokens_here - 1][None, :])

    def chain(earlier_part, later_part):
        return (earlier_part[0] * later_part[0], later_part[0] * earlier_part[1] + later_part[1])

    chain_out = prefix((through, local_end), "context", chain, (jnp.ones_like(through), zero_state))
    incoming = chain_out[1]
    row_group = 32
    group_count = tokens_here // row_group

    def carried_in(operands):
        cumulative_rows, c_group = operands
        decayed = jnp.exp(cumulative_rows[:, None, :] * neg_rate[None, :, :])
        return jnp.sum(c_group[:, :, None] * decayed * incoming[None, :, :], axis=1)

    correction = lax.map(
        carried_in,
        (
            cumulative.reshape(group_count, row_group, cumulative.shape[1]),
            c_rows.reshape(group_count, row_group, c_rows.shape[1]),
        ),
    )
    outputs = local_outputs + correction.reshape(tokens_here, cumulative.shape[1])
    mamba_out = (
        (outputs + skip_gain[None, :] * conved) * jax.nn.silu(z_gate[0].astype(jnp.float32))
    ).astype(jnp.bfloat16)
    mamba_score = jnp.sum(mamba_out.astype(jnp.float32) * mamba_vector[None, :], axis=-1)
    hidden_rows = hidden[0].astype(jnp.float32)
    mean_square = jnp.mean(hidden_rows * hidden_rows, axis=-1, keepdims=True)
    normed = (hidden_rows * lax.rsqrt(mean_square + norm_eps) * norm_gain[None, :]).astype(
        jnp.bfloat16
    )
    axis_experts = lax.axis_size("expert")
    local_experts = expert_gate.shape[0]
    all_experts = axis_experts * local_experts
    capacity = tokens_here * 5 // 64
    expert_ids = jnp.arange(all_experts, dtype=jnp.int32)
    route_rows = routes[0]
    matches = (route_rows[:, :, None] == expert_ids[None, None, :]).astype(jnp.int32)
    chosen = jnp.sum(matches, axis=1) * live_rows[:, None].astype(jnp.int32)
    before = jnp.cumsum(chosen, axis=0) - chosen
    slot_ids = jnp.arange(capacity, dtype=jnp.int32)
    placed = (chosen[:, :, None] == 1) & (before[:, :, None] == slot_ids[None, None, :])
    placed = placed.reshape(tokens_here, axis_experts, local_experts, capacity)
    outgoing = jnp.einsum(
        "tilc,td->licd", placed.astype(jnp.bfloat16), normed, preferred_element_type=jnp.float32
    ).astype(jnp.bfloat16)
    arrived = lax.all_to_all(outgoing, "expert", split_axis=1, concat_axis=1, tiled=True)
    slot_rows = arrived.reshape(local_experts, axis_experts * capacity, normed.shape[1])
    row_piece = lax.all_gather(slot_rows, "context", axis=1, tiled=True)
    gate_part = jnp.einsum(
        "lrd,ldf->lrf", row_piece, expert_gate, preferred_element_type=jnp.float32
    )
    up_part = jnp.einsum("lrd,ldf->lrf", row_piece, expert_up, preferred_element_type=jnp.float32)
    inner_units = (jax.nn.silu(gate_part) * up_part).astype(jnp.bfloat16)
    partial_terms = jnp.sum(inner_units.astype(jnp.float32) * expert_vector[:, None, :], axis=-1)
    slot_values = lax.psum_scatter(partial_terms, "context", scatter_dimension=1, tiled=True)
    returned = lax.all_to_all(
        slot_values.reshape(local_experts, axis_experts, capacity),
        "expert",
        split_axis=1,
        concat_axis=1,
        tiled=True,
    )
    per_expert = jnp.einsum(
        "tilc,lic->til", placed.astype(jnp.float32), returned, precision=lax.Precision.HIGHEST
    ).reshape(tokens_here, all_experts)
    gate_weights = jnp.sum(route_gate[0][:, :, None] * matches.astype(jnp.float32), axis=1)
    expert_score = jnp.sum(per_expert * gate_weights, axis=-1)
    base_score = jnp.sum(hidden_rows * impact_vector[None, :], axis=-1)
    score = base_score + attn_score + mamba_score + expert_score
    impacts = jnp.where(live_rows, jax.nn.relu(score), 0.0)
    shard_count = lax.axis_size("context")
    vocab_block = VOCAB // shard_count
    pooled = jnp.zeros((VOCAB,), jnp.float32).at[term_ids[0]].max(impacts)
    everything = lax.pmax(pooled.astype(jnp.bfloat16), "context").astype(pooled.dtype)
    own_block = lax.dynamic_slice_in_dim(everything, shard_index * vocab_block, vocab_block, 0)
    return (impacts[None, :], own_block[None, :])


def solution(mesh):
    placed = (
        P("expert", "context", None),
        P("expert", "context", None),
        P("expert", "context", None),
        P("expert", "context", None),
        P("expert", "context", None),
        P("expert", "context", None),
        P("expert", "context", None),
        P("expert", "context", None),
        P("expert", "context", None),
        P(),
        P(),
        P(),
        P(),
        P(),
        P(),
        P(),
        P(),
        P(),
        P("expert", None, "context"),
        P("expert", None, "context"),
        P("expert", "context"),
        P("expert", "context", None),
        P("expert", "context", None),
        P(),
        P("expert", "context"),
    )
    return jax.shard_map(
        shards,
        mesh=mesh,
        in_specs=placed,
        out_specs=(P("expert", "context"), P("expert", "context")),
        check_vma=False,
    )
```

profile of v0, /device:TPU:2, one launch (start us, length us, event | category | flops | bytes accessed | tf_op | source)
XLA Modules:
  0.0 1122.7 jit_solution(12694423566203048189)
XLA Ops:
  12.3 3.8 collective-permute-start
  16.1 3.8 compare_select_fusion
  19.9 4.7 reduce_window_sum.22
  31.9 441.6 %while.57 = (s32[]{:T(128)}, f32[16,4096]{1,0:T(8,128)S(1)}, f32[128,4096]{1,0:T(8,128)}, f32[128,4096]{1,0:T(8,128)}, f32[16,4096]{1,0:T(8,128)S(1)}, /*index=5...) while((s32[]{:T(128)}, f32[16,4096]{1,0:T(8,128)S(1)}, ...), condition=%wide.region_8.9_spmd.clone.clone, body=%wide.region_6.8_spmd.clone.sunk.clone | while | flops 458755 | bytes 934379 | solution.py:153
  481.0 15.0 %all_to_all.10 = bf16[2,8,10,2048]{3,0,2,1:T(2,128)(2,1)S(1)} all-to-all(bf16[2,8,10,2048]{3,0,2,1:T(2,128)(2,1)S(1)} %copy.85), channel_id=1, replica_groups=mesh['expert'=8,'context'=32] {'expert'}, dimensions={1} | all-to-all | bytes 1310720 | tf_op jit(solution)/shard_map/all_to_all | solution.py:202
  498.6 122.3 %while.56 = (s32[]{:T(128)}, f32[4,4,128]{2,1,0:T(4,128)S(1)}, f32[4,4,128]{2,1,0:T(4,128)S(1)}, f32[4,4,128,128]{3,2,1,0:T(8,128)}, s32[8]{0:T(128)S(1)}, /*ind...) while((s32[]{:T(128)}, f32[4,4,128]{2,1,0:T(4,128)S(1)}, ...), condition=%wide.region_4.5_spmd.clone.clone, body=%wide.region_1.0_spmd.clone.sunk.clone | while | flops 551365248 | bytes 35525820 | solution.py:122
  503.9 2.8 fusion.97
  506.7 3.3 fusion.98
  517.9 2.8 fusion.97
  520.8 3.3 fusion.98
  524.2 3.7 fusion.100
  533.2 2.8 fusion.97
  536.0 3.4 fusion.98
  539.5 3.7 fusion.100
  551.4 3.3 fusion.98
  554.9 3.7 fusion.100
  566.7 3.3 fusion.98
  570.2 3.8 fusion.100
  582.2 3.4 fusion.98
  585.7 3.7 fusion.100
  597.5 3.4 fusion.98
  601.1 3.7 fusion.100
  612.8 4.0 fusion.98
  617.2 3.7 fusion.100
  623.5 95.9 %all-gather.10.cloned.1.call-done = bf16[2,2560,2048]{2,1,0:T(8,128)(2,1)} async-done(((bf16[2,80,2048]{2,1,0:T(8,128)(2,1)}), bf16[2,2560,2048]{2,1,0:T(8,128)(2,1)}) %all-gather.10.cloned.1.call-update) | async-done | bytes 20971536 | tf_op jit(solution)/shard_map/all_gather | solution.py:204
  719.4 12.7 %fusion.66 = f32[2,2560,224]{1,2,0:T(8,128)} fusion(bf16[2,2560,2048]{2,1,0:T(8,128)(2,1)} %all-gather.10.cloned.1.call-done, bf16[2,2048,224]{1,2,0:T(8,128)(2,1)S(1)} %copy-done), kind=kOutput, calls=%fused_computation.119 | convolution fusion | flops 4697620480 | bytes 27394048 | tf_op jit(solution)/shard_map/lrd,ldf->lrf/dot_general | solution.py:205
  732.1 12.3 %multiply_reduce_fusion.2 = f32[2,2560]{1,0:T(2,128)S(1)} fusion(f32[2,224]{1,0:T(2,128)S(1)} %copy-done.22, bf16[2,2560,2048]{2,1,0:T(8,128)(2,1)} %all-gather.10.cloned.1.call-done, bf16[2,2048,224]{1,2,0:T(8,128)(2,1)} %param.52, f32[2,2560,224]{1,2,0:T(8,128)} %fusion.66), kind=kOutput, calls=%fused_computation.40 | convolution fusion | flops 4707937280 | bytes 27416320 | tf_op jit(solution)/shard_map/lrd,ldf->lrf/dot_general | solution.py:208
  746.0 18.8 %while.55 = (s32[]{:T(128)}, f32[4,32,4096]{2,1,0:T(8,128)}, f32[4,32,16]{1,0,2:T(4,128)S(1)}, f32[4,32,4096]{2,1,0:T(8,128)}, f32[16,4096]{1,0:T(8,128)S(1)}, /*index=5*/f32[16,4096]{1,0:T(8,128)S(1)}) while((s32[]{:T(128)}, f32[4,32,4096]{2,1,0:T(8,128)}, f32[4,32,16]{1,0,2:T(4,128)S(1)}, f32[4,32,4096]{2,1,0:T(8,128)}, ...), condition=%wide.region_14.15_spmd.clone, body=%wide.region_12.14_spmd.sunk.clone | while | flops 8257538 | bytes 3680845 | solution.py:170
  764.8 194.5 %reduce-scatter.4.cloned.1.call-done = f32[80,2]{1,0:T(8,128)} async-done(((f32[2560,2]{1,0:T(8,128)}), f32[80,2]{1,0:T(8,128)}) %reduce-scatter.4.cloned.1.call-update) | async-done | bytes 656
  960.9 4.8 all-to-all-start.1
  965.8 6.5 multiply_reduce_fusion.3
  976.4 138.2 %all-reduce.2.cloned.1.call-done = bf16[65536]{0:T(1024)(128)(2,1)} async-done(((bf16[65536]{0:T(1024)(128)(2,1)}), bf16[65536]{0:T(1024)(128)(2,1)}) %all-reduce.2.cloned.1.call-update) | async-done | bytes 131088 | tf_op jit(solution)/shard_map/pmax | solution.py:230
  (737 shorter events, 536.5 us)
Async XLA Ops:
  7.2 712.3 %copy-start = (bf16[2,2048,224]{1,2,0:T(8,128)(2,1)S(1)}, bf16[2,2048,224]{1,2,0:T(8,128)(2,1)}, u32[]{:S(2)}) copy-start(bf16[2,2048,224]{1,2,0:T(8,128)(2,1)} %param.51) | copy-start | bytes 5505028
  7.2 491.4 %all-gather.12.cloned.1.call-start = ((), (), s32[]{:S(2)}) async-start(), calls=%async_computation.5 | async-start | bytes 4325376 | tf_op jit(solution)/shard_map/all_gather | solution.py:108
  9.0 489.6 %all-gather.14.cloned.1.call-start = ((), (), s32[]{:S(2)}) async-start(), calls=%async_computation.6 | async-start | bytes 4325376 | tf_op jit(solution)/shard_map/all_gather | solution.py:109
  10.8 612.4 %all-gather.16.cloned.1.call-start = ((), (), s32[]{:S(2)}) async-start(), calls=%async_computation.7 | async-start | bytes 4325376 | tf_op jit(solution)/shard_map/all_gather | solution.py:24
  12.3 16.6 %collective-permute-start = (bf16[3,4096]{1,0:T(4,128)(2,1)}, bf16[3,4096]{1,0:T(4,128)(2,1)S(1)}, u32[]{:S(2)}, u32[]{:S(2)}) collective-permute-start(bf16[3,4096]{1,0:T(4,128)(2,1)} %slice_bitcast_fusion), channel_id=1, source_target_pairs={{0,1},{1,2},{2,3},{3,4},{4,5},{5,6},{6,7},{7,8},{8,9},{9,10},{10,1... | collective-permute-start | bytes 73736 | tf_op jit(solution)/shard_map/ppermute | solution.py:18
  19.9 5.7 copy-start.7
  19.9 7.5 copy-start.14
  19.9 8.3 copy-start.9
  19.9 9.0 copy-start.4
  25.6 3.6 copy-start.8
  26.3 596.9 %all-gather.18.cloned.1.call-start = ((), (), s32[]{:S(2)}) async-start(), calls=%async_computation.8 | async-start | bytes 4325376 | tf_op jit(solution)/shard_map/all_gather | solution.py:24
  31.9 442.4 %copy-start.17 = (s32[1,128,2]{1,2,0:T(2,128)S(1)}, s32[1,128,2]{1,2,0:T(2,128)}, u32[]{:S(2)}) copy-start(s32[1,128,2]{1,2,0:T(2,128)} %param.54) | copy-start | bytes 3076
  31.9 442.7 %copy-start.23 = (s32[8]{0:T(128)S(1)}, s32[8]{0:T(128)}, u32[]{:S(2)}) copy-start(s32[8]{0:T(128)} %param.56) | copy-start | bytes 100
  474.2 4.5 copy-start.21
  474.3 245.2 %all-gather.10.cloned.1.call-start = ((), (), s32[]{:S(2)}) async-start(), calls=%async_computation.3 | async-start | bytes 21626880 | tf_op jit(solution)/shard_map/all_gather | solution.py:204
  480.3 17.0 %copy-start.10 = (f32[1,128,16]{1,2,0:T(8,128)S(1)}, f32[1,128,16]{1,2,0:T(8,128)}, u32[]{:S(2)}) copy-start(f32[1,128,16]{1,2,0:T(8,128)} %param.41) | copy-start | bytes 24580
  480.3 17.1 %copy-start.6 = (bf16[1,128,2048]{2,1,0:T(8,128)(2,1)S(1)}, bf16[1,128,2048]{2,1,0:T(8,128)(2,1)}, u32[]{:S(2)}) copy-start(bf16[1,128,2048]{2,1,0:T(8,128)(2,1)} %param.34) | copy-start | bytes 1572868
  497.1 462.2 %reduce-scatter.4.cloned.1.call-start = ((), (), s32[]{:S(2)}) async-start(), calls=%async_computation.9 | async-start | bytes 1351680
  498.6 122.3 %copy-start.13 = (f32[2048]{0:T(1024)S(1)}, f32[2048]{0:T(1024)}, u32[]{:S(2)}) copy-start(f32[2048]{0:T(1024)} %param.48) | copy-start | bytes 24580
  566.7 3.6 copy-start.2
  582.2 3.5 copy-start.2
  597.5 3.5 copy-start.2
  612.8 4.4 copy-start.2
  623.5 108.7 %copy-start.22 = (f32[2,224]{1,0:T(2,128)S(1)}, f32[2,224]{1,0:T(2,128)}, u32[]{:S(2)}) copy-start(f32[2,224]{1,0:T(2,128)} %param.53) | copy-start | bytes 5380
  746.0 219.7 %copy-start.5 = (bf16[1,128,4096]{2,1,0:T(8,128)(2,1)S(1)}, bf16[1,128,4096]{2,1,0:T(8,128)(2,1)}, u32[]{:S(2)}) copy-start(bf16[1,128,4096]{2,1,0:T(8,128)(2,1)} %param.38) | copy-start | bytes 3145732
  746.0 219.7 %copy-start.11 = (f32[4096]{0:T(1024)S(1)}, f32[4096]{0:T(1024)}, u32[]{:S(2)}) copy-start(f32[4096]{0:T(1024)} %param.47) | copy-start | bytes 49156
  960.9 11.4 %all-to-all-start.1 = ((f32[2,8,10]{2,0,1:T(2,128)}), f32[2,8,10]{2,0,1:T(2,128)S(1)}, u32[]{:S(2)}, u32[]{:S(2)}) async-start(f32[2,8,10]{2,0,1:T(2,128)} %copy.87), calls=%async_computation.1 | async-start | bytes 16384 | tf_op jit(solution)/shard_map/all_to_all | solution.py:212
  965.7 148.9 %all-reduce.2.cloned.1.call-start = ((), (), s32[]{:S(2)}) async-start(), calls=%async_computation.4 | async-start | bytes 262144 | tf_op jit(solution)/shard_map/pmax | solution.py:230
  965.7 6.5 copy-start.16
  965.7 6.7 copy-start.18
  965.8 6.7 copy-start.19
  965.8 150.1 %copy-start.1 = (bf16[2,2048,224]{1,2,0:T(8,128)(2,1)S(1)}, bf16[2,2048,224]{1,2,0:T(8,128)(2,1)}, u32[]{:S(2)}) copy-start(bf16[2,2048,224]{1,2,0:T(8,128)(2,1)} %param.51) | copy-start | bytes 5505028
  (9 other events, 27.5 us)
Sparse Core Ops, SparseCore 0:
  10.5 86.1 all-gather.11
  99.1 83.3 all-gather.13
  185.1 81.9 all-gather.15
  474.4 83.8 all-gather.17
  560.8 158.6 all-gather.9
  746.1 213.1 reduce-scatter.3
  975.4 139.1 all-reduce.1
where the time goes:
time: 1130 us; the launch traced here: 1120 us
  waiting for transfers between devices  429 us (38%)
  local copies, waits for them, and re-layouts  340 us (30%)
  other arithmetic  220 us (19%)
  matrix products  77.8 us (7%)
  loops' own time  17.7 us (2%)
  blocking collectives  15 us (1%)
  between operations  14.6 us (1%)
    dynamic_update_slice x128, local copies, waits for them, and re-layouts, shards(): lax.scan(emit_rows, zero_state, (step_size, b_rows, c_rows, conved))  207 us
    unnamed x8, waiting for transfers between devices  195 us
    pmax x1, waiting for transfers between devices, shards(): lax.pmax(pooled.astype(jnp.bfloat16), 'context').astype(pooled.dtype)  138 us
    dynamic_slice x128, other arithmetic, shards(): lax.scan(emit_rows, zero_state, (step_size, b_rows, c_rows, conved))  127 us
    all_gather x1, waiting for transfers between devices, shards(): row_piece = lax.all_gather(slot_rows, 'context', axis=1, tiled=True)  95.9 us
    mul x128, local copies, waits for them, and re-layouts, emit_rows(): (size_now * x_now)[None, :] * b_now[:, None]  89 us
    dot_general x8, matrix products, key_block(): jnp.einsum('gqtr,rgd->gqtd', exp_scores.astype(jnp.bfloat16), value_heads...  28.6 us
    reduce_sum x8, other arithmetic, key_block(): running_sum = running_sum * factor + jnp.sum(exp_scores, axis=-1)  27.5 us
  transfers between devices with their start and end apart: 9, of which 3 were waited for; matrix products, arithmetic and copies ran while one was open for 54% of the time, Pallas kernels for 0%

commit v1 on v0

--- a/solution.py
+++ b/solution.py
@@ -201,7 +201,9 @@
     ).astype(jnp.bfloat16)
     arrived = lax.all_to_all(outgoing, "expert", split_axis=1, concat_axis=1, tiled=True)
     slot_rows = arrived.reshape(local_experts, axis_experts * capacity, normed.shape[1])
-    row_piece = lax.all_gather(slot_rows, "context", axis=1, tiled=True)
+    row_piece = jnp.concatenate(
+        lax.all_to_all(jnp.stack([slot_rows] * lax.axis_size("context")), "context", 0, 0), axis=1
+    )
     gate_part = jnp.einsum(
         "lrd,ldf->lrf", row_piece, expert_gate, preferred_element_type=jnp.float32
     )

time: 1130 us -> 1180 us (1.044)
  waiting for transfers between devices: 429 us -> 548 us
  local copies, waits for them, and re-layouts: 340 us -> 278 us
  starting transfers between devices: 9.09 us -> 24.6 us
  blocking collectives: 15 us -> 0 us
    all_gather x2, waiting for transfers between devices: 0.01 us -> 182 us  [prefix(): lax.all_gather(a.astype(kind), axis)]
    all_gather x1 -> x0, waiting for transfers between devices: 95.9 us -> none  [shards(): row_piece = lax.all_gather(slot_rows, 'context', axis=1, tiled=True)]
    mul x128, local copies, waits for them, and re-layouts: 89 us -> 1.68 us  [emit_rows(): (size_now * x_now)[None, :] * b_now[:, None]]
    unnamed x8 -> x7, waiting for transfers between devices: 195 us -> 227 us
    all_to_all x0 -> x2, starting transfers between devices: none -> 17.1 us  [the longest x1 10.7 us: shards(): lax.all_to_all(jnp.stack([slot_rows] * lax.axis_size('context')), 'contex...]
    reshape x1, local copies, waits for them, and re-layouts: 1.08 us -> 17.6 us  [shards(): jnp.concatenate(lax.all_to_all(jnp.stack([slot_rows] * lax.axis_size('con...]
    all_to_all x1 -> x0, blocking collectives: 15 us -> none  [shards(): lax.all_to_all(outgoing, 'expert', split_axis=1, concat_axis=1, tiled=True)]
  transfers between devices with their start and end apart: 9 -> 10, of which waited for: 3 -> 4; matrix products, arithmetic and copies ran while one was open for 54% -> 44% of each run, Pallas kernels for 0% -> 0%
where the time goes in v1:
time: 1180 us
  waiting for transfers between devices  548 us (46%)
  local copies, waits for them, and re-layouts  278 us (24%)
  other arithmetic  217 us (18%)
  matrix products  76.3 us (6%)
  starting transfers between devices  24.6 us (2%)
  loops' own time  18.4 us (2%)
  between operations  14.6 us (1%)
    unnamed x7, waiting for transfers between devices  227 us
    dynamic_update_slice x128, local copies, waits for them, and re-layouts, shards(): lax.scan(emit_rows, zero_state, (step_size, b_rows, c_rows, conved))  207 us
    all_gather x2, waiting for transfers between devices, prefix(): lax.all_gather(a.astype(kind), axis)  182 us
    pmax x1, waiting for transfers between devices, shards(): lax.pmax(pooled.astype(jnp.bfloat16), 'context').astype(pooled.dtype)  138 us
    dynamic_slice x128, other arithmetic, shards(): lax.scan(emit_rows, zero_state, (step_size, b_rows, c_rows, conved))  127 us
    dot_general x8, matrix products, key_block(): jnp.einsum('gqtr,rgd->gqtd', exp_scores.astype(jnp.bfloat16), value_heads...  28.4 us
    reduce_sum x8, other arithmetic, key_block(): running_sum = running_sum * factor + jnp.sum(exp_scores, axis=-1)  26.7 us
  transfers between devices with their start and end apart: 10, of which 4 were waited for; matrix products, arithmetic and copies ran while one was open for 44% of the time, Pallas kernels for 0%

profile of v1, /device:TPU:2, one launch (start us, length us, event | category | flops | bytes accessed | tf_op | source)
XLA Modules:
  0.0 1177.4 jit_solution(16427792794597735197)
XLA Ops:
  17.1 6.4 all-to-all-start
  29.3 4.7 reduce_window_sum.22
  45.4 7.4 stack.3
  52.8 10.7 all-to-all-start.1
  63.6 355.8 %while.57 = (s32[]{:T(128)}, f32[16,4096]{1,0:T(8,128)S(1)}, f32[128,4096]{1,0:T(8,128)}, f32[128,4096]{1,0:T(8,128)}, f32[16,4096]{1,0:T(8,128)S(1)}, /*index=5...) while((s32[]{:T(128)}, f32[16,4096]{1,0:T(8,128)S(1)}, ...), condition=%wide.region_8.9_spmd.clone.clone, body=%wide.region_6.8_spmd.clone.sunk.clone | while | flops 458755 | bytes 934379 | solution.py:153
  420.3 119.1 %while.56 = (s32[]{:T(128)}, f32[4,4,128]{2,1,0:T(4,128)S(1)}, f32[4,4,128]{2,1,0:T(4,128)S(1)}, f32[4,4,128,128]{3,2,1,0:T(8,128)}, s32[8]{0:T(128)S(1)}, /*ind...) while((s32[]{:T(128)}, f32[4,4,128]{2,1,0:T(4,128)S(1)}, ...), condition=%wide.region_4.5_spmd.clone.clone, body=%wide.region_1.0_spmd.clone.sunk.clone | while | flops 551365248 | bytes 35525820 | solution.py:122
  428.3 3.3 fusion.98
  442.1 3.3 fusion.98
  445.5 3.7 fusion.100
  457.1 3.3 fusion.98
  460.6 3.7 fusion.100
  472.2 3.3 fusion.98
  475.6 3.7 fusion.100
  484.4 2.8 fusion.97
  487.2 3.3 fusion.98
  490.7 3.7 fusion.100
  502.3 3.3 fusion.98
  505.7 3.7 fusion.100
  517.3 3.4 fusion.98
  520.8 3.7 fusion.100
  532.3 3.3 fusion.98
  535.8 3.7 fusion.100
  541.1 100.9 %all-gather.13.cloned.1.call-done = bf16[512,4096]{1,0:T(8,128)(2,1)} async-done(((bf16[16,4096]{1,0:T(8,128)(2,1)}), bf16[512,4096]{1,0:T(8,128)(2,1)}) %all-gather.13.cloned.1.call-update) | async-done | bytes 4194320 | tf_op jit(solution)/shard_map/all_gather | solution.py:24
  642.0 81.5 %all-gather.15.cloned.1.call-done = bf16[512,4096]{1,0:T(8,128)(2,1)} async-done(((bf16[16,4096]{1,0:T(8,128)(2,1)}), bf16[512,4096]{1,0:T(8,128)(2,1)}) %all-gather.15.cloned.1.call-update) | async-done | bytes 4194320 | tf_op jit(solution)/shard_map/all_gather | solution.py:24
  723.6 17.6 %copy.88 = bf16[2,32,80,2048]{3,2,1,0:T(8,128)(2,1)} copy(bf16[2,32,80,2048]{3,2,0,1:T(8,128)(2,1)} %bitcast.34) | data formatting | bytes 41943040 | tf_op jit(solution)/shard_map/reshape | solution.py:204
  741.2 12.6 %fusion.66 = f32[2,2560,224]{1,2,0:T(8,128)} fusion(bf16[2,2560,2048]{2,1,0:T(8,128)(2,1)} %bitcast.185, bf16[2,2048,224]{1,2,0:T(8,128)(2,1)S(1)} %copy-done), kind=kOutput, calls=%fused_computation.119 | convolution fusion | flops 4697620480 | bytes 27394048 | tf_op jit(solution)/shard_map/lrd,ldf->lrf/dot_general | solution.py:207
  753.9 12.3 %multiply_reduce_fusion.2 = f32[2,2560]{1,0:T(2,128)S(1)} fusion(f32[2,224]{1,0:T(2,128)S(1)} %copy-done.20, bf16[2,2560,2048]{2,1,0:T(8,128)(2,1)} %bitcast.186, bf16[2,2048,224]{1,2,0:T(8,128)(2,1)} %param.52, f32[2,2560,224]{1,2,0:T(8,128)} %fusion.66), kind=kOutput, calls=%fused_computation.40 | convolution fusion | flops 4707937280 | bytes 27416320 | tf_op jit(solution)/shard_map/lrd,ldf->lrf/dot_general | solution.py:210
  767.8 18.8 %while.55 = (s32[]{:T(128)}, f32[4,32,4096]{2,1,0:T(8,128)}, f32[4,32,16]{1,0,2:T(4,128)S(1)}, f32[4,32,4096]{2,1,0:T(8,128)}, f32[16,4096]{1,0:T(8,128)S(1)}, /*index=5*/f32[16,4096]{1,0:T(8,128)S(1)}) while((s32[]{:T(128)}, f32[4,32,4096]{2,1,0:T(8,128)}, f32[4,32,16]{1,0,2:T(4,128)S(1)}, f32[4,32,4096]{2,1,0:T(8,128)}, ...), condition=%wide.region_14.15_spmd.clone, body=%wide.region_12.14_spmd.sunk.clone | while | flops 8257538 | bytes 3680845 | solution.py:170
  786.6 227.3 %reduce-scatter.4.cloned.1.call-done = f32[80,2]{1,0:T(8,128)} async-done(((f32[2560,2]{1,0:T(8,128)}), f32[80,2]{1,0:T(8,128)}) %reduce-scatter.4.cloned.1.call-update) | async-done | bytes 656
  1015.4 4.9 all-to-all-start.2
  1020.3 6.8 multiply_reduce_fusion.3
  1031.3 138.0 %all-reduce.2.cloned.1.call-done = bf16[65536]{0:T(1024)(128)(2,1)} async-done(((bf16[65536]{0:T(1024)(128)(2,1)}), bf16[65536]{0:T(1024)(128)(2,1)}) %all-reduce.2.cloned.1.call-update) | async-done | bytes 131088 | tf_op jit(solution)/shard_map/pmax | solution.py:232
  (733 shorter events, 458.0 us)
Async XLA Ops:
  7.2 734.1 %copy-start = (bf16[2,2048,224]{1,2,0:T(8,128)(2,1)S(1)}, bf16[2,2048,224]{1,2,0:T(8,128)(2,1)}, u32[]{:S(2)}) copy-start(bf16[2,2048,224]{1,2,0:T(8,128)(2,1)} %param.51) | copy-start | bytes 5505028
  7.2 7.6 copy-start.5
  7.2 7.6 copy-start.14
  7.2 413.1 %all-gather.9.cloned.1.call-start = ((), (), s32[]{:S(2)}) async-start(), calls=%async_computation.5 | async-start | bytes 4325376 | tf_op jit(solution)/shard_map/all_gather | solution.py:108
  9.1 411.2 %all-gather.11.cloned.1.call-start = ((), (), s32[]{:S(2)}) async-start(), calls=%async_computation.6 | async-start | bytes 4325376 | tf_op jit(solution)/shard_map/all_gather | solution.py:109
  10.8 4.3 copy-start.19
  15.6 11.1 copy-start.4
  15.6 11.1 copy-start.11
  17.1 27.0 %all-to-all-start = ((bf16[2,8,10,2048]{3,0,2,1:T(2,128)(2,1)}), bf16[2,8,10,2048]{3,0,2,1:T(2,128)(2,1)}, u32[]{:S(2)}, u32[]{:S(2)}) async-start(bf16[2,8,10,2048]{3,0,2,1:T(2,128)(2,1)} %copy.86), calls=%async_computation | async-start | bytes 1310720 | tf_op jit(solution)/shard_map/all_to_all | solution.py:202
  23.5 618.5 %all-gather.13.cloned.1.call-start = ((), (), s32[]{:S(2)}) async-start(), calls=%async_computation.7 | async-start | bytes 4325376 | tf_op jit(solution)/shard_map/all_gather | solution.py:24
  24.4 14.2 %collective-permute-start = (bf16[3,4096]{1,0:T(4,128)(2,1)S(1)}, bf16[3,4096]{1,0:T(4,128)(2,1)S(1)}, u32[]{:S(2)}, u32[]{:S(2)}) collective-permute-start(bf16[3,4096]{1,0:T(4,128)(2,1)S(1)} %slice_bitcast_fusion), channel_id=1, source_target_pairs={{0,1},{1,2},{2,3},{3,4},{4,5},{5,6},{6,7},{7,8},{8,9},{9,10},{10,1... | collective-permute-start | bytes 73736 | tf_op jit(solution)/shard_map/ppermute | solution.py:18
  29.2 5.7 copy-start.7
  29.2 6.4 copy-start.17
  29.2 6.5 copy-start.18
  29.2 6.5 copy-start.9
  29.2 6.5 copy-start.21
  29.3 6.6 copy-start.10
  29.3 6.8 copy-start.16
  29.3 6.9 copy-start.6
  37.2 4.3 copy-start.8
  52.8 670.8 %all-to-all-start.1 = ((bf16[32,2,80,2048]{3,2,1,0:T(8,128)(2,1)}), bf16[32,2,80,2048]{3,2,1,0:T(8,128)(2,1)}, u32[]{:S(2)}, u32[]{:S(2)}) async-start(bf16[32,2,80,2048]{3,2,1,0:T(8,128)(2,1)} %stack.3), calls=%async_computation.1 | async-start | bytes 41943040 | tf_op jit(solution)/shard_map/all_to_all | solution.py:205
  63.5 660.0 %all-gather.15.cloned.1.call-start = ((), (), s32[]{:S(2)}) async-start(), calls=%async_computation.8 | async-start | bytes 4325376 | tf_op jit(solution)/shard_map/all_gather | solution.py:24
  420.0 593.8 %reduce-scatter.4.cloned.1.call-start = ((), (), s32[]{:S(2)}) async-start(), calls=%async_computation.9 | async-start | bytes 1351680
  420.3 119.2 %copy-start.15 = (f32[2048]{0:T(1024)S(1)}, f32[2048]{0:T(1024)}, u32[]{:S(2)}) copy-start(f32[2048]{0:T(1024)} %param.48) | copy-start | bytes 24580
  517.3 3.5 copy-start.2
  532.3 3.5 copy-start.2
  741.2 12.6 %copy-start.20 = (f32[2,224]{1,0:T(2,128)S(1)}, f32[2,224]{1,0:T(2,128)}, u32[]{:S(2)}) copy-start(f32[2,224]{1,0:T(2,128)} %param.53) | copy-start | bytes 5380
  767.7 252.5 %copy-start.12 = (f32[4096]{0:T(1024)S(1)}, f32[4096]{0:T(1024)}, u32[]{:S(2)}) copy-start(f32[4096]{0:T(1024)} %param.47) | copy-start | bytes 49156
  767.8 252.5 %copy-start.13 = (f32[4096]{0:T(1024)S(1)}, f32[4096]{0:T(1024)}, u32[]{:S(2)}) copy-start(f32[4096]{0:T(1024)} %param.46) | copy-start | bytes 49156
  1015.4 11.7 all-to-all-start.2
  1020.3 149.0 %all-reduce.2.cloned.1.call-start = ((), (), s32[]{:S(2)}) async-start(), calls=%async_computation.4 | async-start | bytes 262144 | tf_op jit(solution)/shard_map/pmax | solution.py:232
  1020.3 150.3 %copy-start.1 = (bf16[2,2048,224]{1,2,0:T(8,128)(2,1)S(1)}, bf16[2,2048,224]{1,2,0:T(8,128)(2,1)}, u32[]{:S(2)}) copy-start(bf16[2,2048,224]{1,2,0:T(8,128)(2,1)} %param.51) | copy-start | bytes 5505028
  (7 other events, 22.1 us)
Sparse Core Ops, SparseCore 0:
  10.5 159.2 all-gather.8
  172.3 247.4 all-gather.10
  422.4 219.5 all-gather.12
  644.5 79.0 all-gather.14
  767.9 245.9 reduce-scatter.3
  1030.2 139.0 all-reduce.1
